TPU v7x, 32 devices: a whole 2x2x4 slice. The times are simulated.
32 devices in a mesh: row: 8 (over z, x), col: 4 (over y, core).
Axes of the slice: x: 2, y: 2, z: 4, core: 2. Of those that a mesh axis runs over, the one named last changes fastest.
Arguments:
- stream: bfloat16 [384, 8192], P('row', 'col'), may hold values from -6 to 6
- attention_gain: bfloat16 [8192], P('col'), may hold values from 0.25 to 1.75
- query_weight: bfloat16 [8192, 8192], P('col', 'row'), may hold values from -1 to 1
- pair_weight: bfloat16 [8192, 2048], P('col'), may hold values from -1 to 1
- out_weight: bfloat16 [8192, 8192], P('row', 'col'), may hold values from -0.0625 to 0.0625
- unit_gain: bfloat16 [8192], P('col'), may hold values from 0.25 to 1.75
- gate_weight: bfloat16 [8192, 24576], P('col', 'row'), may hold values from -0.0625 to 0.0625
- up_weight: bfloat16 [8192, 24576], P('col', 'row'), may hold values from -0.0625 to 0.0625
- down_weight: bfloat16 [24576, 8192], P('row', 'col'), may hold values from -0.0390625 to 0.0390625
Outputs:
- layer_out: bfloat16 [384, 8192], P('row', 'col')
All inputs are finite; a program needn't handle non-finite values.
Results may differ from a plain program's by a relative error of at most 0.028.
Values may be sent and summed in bfloat16 or wider, within the bound.
A program may use at most 128 MiB of HBM per device.

v0:
```python
import jax
import jax.numpy as jnp
from jax import lax
from jax.sharding import PartitionSpec as P

D = 8192
HEADS = 64
KV_HEADS = 8
HD = 128


rope_base = 500000.0
epsilon = 1e-05


def rotate(values, positions):
    half_width = values.shape[-1] // 2
    frequency = rope_base ** (-(jnp.arange(half_width, dtype=jnp.float32) * 2.0 / values.shape[-1]))
    angles = positions.astype(jnp.float32)[:, None] * frequency[None, :]
    cosine = jnp.cos(angles)[:, None, :]
    sine_part = jnp.sin(angles)[:, None, :]
    first_part = values[..., :half_width]
    second = values[..., half_width:]
    return jnp.concatenate(
        [first_part * cosine - second * sine_part, second * cosine + first_part * sine_part],
        axis=-1,
    )


def gather_rows(local_part):
    return lax.all_gather(local_part, "row", axis=0, tiled=True)


def gather_columns(local_part):
    return lax.all_gather(local_part, "col", axis=0, tiled=True)


def row_totals(left_side, weight):
    return lax.psum_scatter(
        jnp.dot(left_side, weight, preferred_element_type=jnp.float32).astype(jnp.bfloat16),
        "row",
        scatter_dimension=0,
        tiled=True,
    ).astype(jnp.float32)


def on_device(
    stream,
    attention_gain,
    query_weight,
    pair_weight,
    out_weight,
    unit_gain,
    gate_weight,
    up_weight,
    down_weight,
):
    row_index = lax.axis_index("row")
    column_index = lax.axis_index("col")
    every_token = gather_rows(stream)
    tokens = every_token.shape[0]
    query_count = tokens // lax.axis_size("col")
    heads_here = query_weight.shape[1] // HD
    query_width = heads_here * HD
    pair_head = row_index * heads_here // (HEADS // KV_HEADS)
    whole_float = every_token.astype(jnp.float32)
    normed = (whole_float * attention_gain.astype(jnp.float32)).astype(jnp.bfloat16)
    pair_columns = lax.dynamic_slice_in_dim(pair_weight, pair_head * 2 * HD, 2 * HD, 1)
    query_part = jnp.dot(normed, query_weight, preferred_element_type=jnp.float32)
    pair_part = jnp.dot(normed, pair_columns, preferred_element_type=jnp.float32)
    token_squares = jnp.sum(whole_float * whole_float, axis=1)
    query_start = column_index * query_count
    query_full, pair_sums, squares = lax.psum((query_part, pair_part, token_squares), "col")
    query_rows = lax.dynamic_slice_in_dim(query_full, query_start, query_count, 0)
    attention_scale = lax.rsqrt(squares / D + epsilon)[:, None]
    positions = jnp.arange(tokens, dtype=jnp.int32)
    row_scale = lax.dynamic_slice_in_dim(attention_scale, query_start, query_count, 0)
    query_positions = query_start + jnp.arange(query_count, dtype=jnp.int32)
    queries = rotate((row_scale * query_rows).reshape(query_count, heads_here, HD), query_positions)
    pair_values = attention_scale * pair_sums
    key_rows = rotate(pair_values[:, :HD].reshape(tokens, 1, HD), positions)[:, 0, :]
    value_rows = pair_values[:, HD:].astype(jnp.bfloat16)
    scores = jnp.einsum("qhd,kd->hqk", queries, key_rows, precision=lax.Precision.HIGHEST) * HD ** (
        -0.5
    )
    causal = query_positions[:, None] >= positions[None, :]
    scores = jnp.where(causal[None, :, :], scores, -1e30)
    largest = jnp.max(scores, axis=-1, keepdims=True)
    exponent = jnp.exp(scores - largest)
    attention = (exponent / jnp.sum(exponent, axis=-1, keepdims=True)).astype(jnp.bfloat16)
    mixture = jnp.einsum("hqk,kd->qhd", attention, value_rows, preferred_element_type=jnp.float32)
    heads_out = mixture.reshape(query_count, query_width).astype(jnp.bfloat16)
    every_head = gather_columns(heads_out)
    attention_rows = row_totals(every_head, out_weight)
    hidden_rows = (stream.astype(jnp.float32) + attention_rows).astype(jnp.bfloat16)
    hidden_all = gather_rows(hidden_rows)
    hidden_float = hidden_all.astype(jnp.float32)
    unit_input = (hidden_float * unit_gain.astype(jnp.float32)).astype(jnp.bfloat16)
    unit_width = gate_weight.shape[1]
    unit_sums = jnp.concatenate(
        [
            jnp.dot(unit_input, gate_weight, preferred_element_type=jnp.float32),
            jnp.dot(unit_input, up_weight, preferred_element_type=jnp.float32),
        ],
        axis=1,
    )
    hidden_squares = jnp.sum(hidden_float * hidden_float, axis=1)
    unit_rows, square_rows = (
        lax.psum_scatter(unit_sums, "col", scatter_dimension=0, tiled=True),
        lax.psum_scatter(hidden_squares, "col", scatter_dimension=0, tiled=True),
    )
    unit_scale = lax.rsqrt(square_rows / D + epsilon)[:, None]
    gate_sums = unit_scale * unit_rows[:, :unit_width]
    upward = unit_scale * unit_rows[:, unit_width:]
    activated = gather_columns((jax.nn.silu(gate_sums) * upward).astype(jnp.bfloat16))
    down_rows = row_totals(activated, down_weight)
    return (hidden_rows.astype(jnp.float32) + down_rows).astype(jnp.bfloat16)


def solution(mesh):
    return jax.shard_map(
        on_device,
        mesh=mesh,
        in_specs=(
            P("row", "col"),
            P("col"),
            P("col", "row"),
            P("col", None),
            P("row", "col"),
            P("col"),
            P("col", "row"),
            P("col", "row"),
            P("row", "col"),
        ),
        out_specs=P("row", "col"),
        check_vma=False,
    )
```

profile of v0, /device:TPU:0, one launch (start us, length us, event | category | flops | bytes accessed | tf_op | source)
XLA Modules:
  0.0 453.4 jit_solution(12776711594681717109)
XLA Ops:
  6.5 0.0 all-gather.4.cloned.1.call-start
  6.5 0.7 all-gather.4.cloned.1.call-update
  7.3 0.0 all-reduce.4.cloned.1.call-start
  7.3 0.7 convert_element_type.80
  8.0 48.4 %all-gather.4.cloned.1.call-done = bf16[384,2048]{1,0:T(8,128)(2,1)} async-done(((bf16[48,2048]{1,0:T(8,128)(2,1)}), bf16[384,2048]{1,0:T(8,128)(2,1)}) %all-gather.4.cloned.1.call-update) | async-done | bytes 1572880 | tf_op jit(solution)/shard_map/all_gather | solution.py:31
  56.4 0.0 copy-start.1
  56.5 5.7 %fusion.13 = f32[384,1024]{1,0:T(8,128)} fusion(bf16[2048,1024]{1,0:T(8,128)(2,1)} %param.11, bf16[384,2048]{1,0:T(8,128)(2,1)} %all-gather.4.cloned.1.call-done, f32[2048]{0:T(1024)S(1)} %convert_element_type.80), kind=kOutput, calls=%fused_computation.19 | convolution fusion | flops 1612972032 | bytes 7348224 | tf_op jit(solution)/shard_map/dot_general | solution.py:69
  62.2 0.0 copy-done.1
  62.2 2.5 fusion.15
  64.7 0.0 all-reduce.4.cloned.1.call-update
  64.8 0.0 reduce-scatter.4.cloned.1.call-start
  64.8 0.1 iota_compare_fusion
  64.9 0.2 multiply_cosine_fusion.1
  65.2 0.4 fusion.1
  65.6 5.7 %psum.21 = f32[384]{0:T(512)S(1)} all-reduce(f32[384]{0:T(512)S(1)} %fusion.1), channel_id=1, replica_groups=mesh['row'=8,'col'=4] {'col'}, use_global_device_ids=true, to_apply=%region_1.2 | all-reduce | flops 384 | bytes 3072 | tf_op jit(solution)/shard_map/psum | solution.py:73
  71.2 0.1 dynamic-slice.3
  71.3 41.2 %all-reduce.4.cloned.1.call-done = (f32[384,1024]{1,0:T(8,128)}, f32[384,256]{1,0:T(8,128)}) async-done(((f32[384,1024]{1,0:T(8,128)}, f32[384,256]{1,0:T(8,128)}), (f32[384,1024]{1,0:T(8,128)}, f32[384,256]{1,0:T(8,128)})) %all-reduce.4.cloned.1.call-update) | async-done | bytes 1966096 | tf_op jit(solution)/shard_map/psum | solution.py:73
  112.5 0.0 copy-start.5
  112.5 1.1 multiply_bitcast_fusion
  113.7 0.1 copy.21
  113.8 0.0 copy-done.5
  113.8 0.1 broadcast_multiply_fusion
  113.9 0.2 fusion.40
  114.1 0.8 fusion.28
  114.9 0.1 multiply_subtract_fusion
  115.1 1.2 fusion.8
  116.3 0.4 fusion.41
  116.7 1.6 fusion.19
  118.3 8.0 %all_gather.13 = bf16[384,1024]{1,0:T(8,128)(2,1)S(1)} all-gather(bf16[96,1024]{1,0:T(8,128)(2,1)S(1)} %bitcast.33), channel_id=1, replica_groups=mesh['row'=8,'col'=4] {'col'}, dimensions={0}, use_global_device_ids=true | all-gather | bytes 983040 | tf_op jit(solution)/shard_map/all_gather | solution.py:35
  126.3 5.2 %convolution_convert_fusion = bf16[384,2048]{1,0:T(8,128)(2,1)} fusion(bf16[384,1024]{1,0:T(8,128)(2,1)S(1)} %all_gather.13, bf16[1024,2048]{1,0:T(8,128)(2,1)} %param.13), kind=kOutput, calls=%fused_computation.10 | convolution fusion | flops 1611399168 | bytes 6553600 | tf_op jit(solution)/shard_map/dot_general | solution.py:40
  131.5 0.0 copy-start.4
  131.5 0.0 copy-start.6
  131.5 0.0 reduce-scatter.4.cloned.1.call-update
  131.5 0.0 all-gather.6.cloned.1.call-start
  131.5 66.5 %reduce-scatter.4.cloned.1.call-done = bf16[48,2048]{1,0:T(8,128)(2,1)} async-done(((bf16[384,2048]{1,0:T(8,128)(2,1)}), bf16[48,2048]{1,0:T(8,128)(2,1)}) %reduce-scatter.4.cloned.1.call-update) | async-done | bytes 196624 | tf_op jit(solution)/shard_map/reduce_scatter | solution.py:39
  198.0 0.0 copy-done.4
  198.0 1.6 add_convert_fusion.1
  199.6 0.0 all-gather.6.cloned.1.call-update
  199.7 0.2 reduce-scatter.6.cloned.1.call-start
  199.9 0.0 copy-done.6
  199.9 43.2 %all-gather.6.cloned.1.call-done = bf16[384,2048]{1,0:T(8,128)(2,1)} async-done(((bf16[48,2048]{1,0:T(8,128)(2,1)}), bf16[384,2048]{1,0:T(8,128)(2,1)}) %all-gather.6.cloned.1.call-update) | async-done | bytes 1572880 | tf_op jit(solution)/shard_map/all_gather | solution.py:31
  243.1 0.0 copy-start.2
  243.1 10.1 %fusion.9 = f32[384,3072]{1,0:T(8,128)S(1)} fusion(bf16[2048,3072]{1,0:T(8,128)(2,1)} %param.16, bf16[384,2048]{1,0:T(8,128)(2,1)} %all-gather.6.cloned.1.call-done, f32[2048]{0:T(1024)S(1)} %convert_element_type.93), kind=kOutput, calls=%fused_computation.17 | convolution fusion | flops 4834197504 | bytes 18882560 | tf_op jit(solution)/shard_map/dot_general | solution.py:103
  253.2 0.0 copy-done.2
  253.2 8.1 %fusion.11 = f32[384,3072]{1,0:T(8,128)S(1)} fusion(bf16[2048,3072]{1,0:T(8,128)(2,1)} %param.15, bf16[384,2048]{1,0:T(8,128)(2,1)S(1)} %copy-done.2, f32[2048]{0:T(1024)S(1)} %convert_element_type.93), kind=kOutput, calls=%fused_computation.18 | convolution fusion | flops 4834197504 | bytes 18882560 | tf_op jit(solution)/shard_map/dot_general | solution.py:102
  261.3 4.7 %pad_maximum_fusion = f32[384,6144]{1,0:T(8,128)} fusion(f32[384,3072]{1,0:T(8,128)S(1)} %fusion.9, f32[384,3072]{1,0:T(8,128)S(1)} %fusion.11), kind=kLoop, calls=%fused_computation.1 | loop fusion | flops 2359296 | bytes 18874368 | tf_op jit(solution)/shard_map/concatenate | solution.py:100
  266.0 0.0 reduce-scatter.6.cloned.1.call-update
  266.0 0.0 all-gather.8.cloned.1.call-start
  266.1 0.6 copy-done.7
  266.7 0.6 dynamic-slice.4
  267.9 0.0 copy-done.3
  267.9 0.4 fusion.3
  268.3 5.7 %all-reduce = f32[384]{0:T(512)S(1)} all-reduce(f32[384]{0:T(512)S(1)} %fusion.3), channel_id=3, replica_groups=mesh['row'=8,'col'=4] {'col'}, use_global_device_ids=true, to_apply=%region_8.9.clone | all-reduce | flops 384 | bytes 3072
  274.0 0.1 fusion.36
  274.0 68.4 %reduce-scatter.6.cloned.1.call-done = f32[96,6144]{1,0:T(8,128)} async-done(((f32[384,6144]{1,0:T(8,128)}), f32[96,6144]{1,0:T(8,128)}) %reduce-scatter.6.cloned.1.call-update) | async-done | bytes 2359312 | tf_op jit(solution)/shard_map/reduce_scatter | solution.py:109
  342.5 2.8 fusion.18
  345.3 0.0 all-gather.8.cloned.1.call-update
  345.3 0.0 reduce-scatter.8.cloned.1.call-start
  345.4 24.2 %all-gather.8.cloned.1.call-done = bf16[384,3072]{1,0:T(8,128)(2,1)} async-done(((bf16[96,3072]{1,0:T(8,128)(2,1)}), bf16[384,3072]{1,0:T(8,128)(2,1)}) %all-gather.8.cloned.1.call-update) | async-done | bytes 2359312 | tf_op jit(solution)/shard_map/all_gather | solution.py:35
  369.5 9.6 %convolution_convert_fusion.1 = bf16[384,2048]{1,0:T(8,128)(2,1)} fusion(bf16[384,3072]{1,0:T(8,128)(2,1)} %all-gather.8.cloned.1.call-done, bf16[3072,2048]{1,0:T(8,128)(2,1)} %param.17), kind=kOutput, calls=%fused_computation.11 | convolution fusion | flops 4832624640 | bytes 16515072 | tf_op jit(solution)/shard_map/dot_general | solution.py:40
  379.2 0.0 reduce-scatter.8.cloned.1.call-update
  379.2 65.8 %reduce-scatter.8.cloned.1.call-done = bf16[48,2048]{1,0:T(8,128)(2,1)} async-done(((bf16[384,2048]{1,0:T(8,128)(2,1)}), bf16[48,2048]{1,0:T(8,128)(2,1)}) %reduce-scatter.8.cloned.1.call-update) | async-done | bytes 196624 | tf_op jit(solution)/shard_map/reduce_scatter | solution.py:39
  444.9 0.0 copy-done
  444.9 1.6 add_convert_fusion
  (10 shorter events, 0.1 us)
Async XLA Ops:
  6.5 49.9 %all-gather.4.cloned.1.call-start = ((), (), s32[]{:S(2)}) async-start(), calls=%async_computation.3 | async-start | bytes 1769472 | tf_op jit(solution)/shard_map/all_gather | solution.py:31
  7.3 105.3 %all-reduce.4.cloned.1.call-start = ((), (), s32[]{:S(2)}) async-start(), calls=%async_computation.9 | async-start | bytes 3932160 | tf_op jit(solution)/shard_map/psum | solution.py:73
  56.4 5.7 %copy-start.1 = (bf16[384,2048]{1,0:T(8,128)(2,1)S(1)}, bf16[384,2048]{1,0:T(8,128)(2,1)}, u32[]{:S(2)}) copy-start(bf16[384,2048]{1,0:T(8,128)(2,1)} %all-gather.4.cloned.1.call-done) | copy-start | bytes 4718596
  64.8 133.2 %reduce-scatter.4.cloned.1.call-start = ((), (), s32[]{:S(2)}) async-start(), calls=%async_computation.4 | async-start | bytes 1769472 | tf_op jit(solution)/shard_map/reduce_scatter | solution.py:39
  112.5 1.2 copy-start.5
  131.5 66.5 %copy-start.4 = (bf16[48,2048]{1,0:T(8,128)(2,1)S(1)}, bf16[48,2048]{1,0:T(8,128)(2,1)}, u32[]{:S(2)}) copy-start(bf16[48,2048]{1,0:T(8,128)(2,1)} %param.9) | copy-start | bytes 589828
  131.5 68.4 %copy-start.6 = (bf16[2048]{0:T(1024)(128)(2,1)S(1)}, bf16[2048]{0:T(1024)(128)(2,1)}, u32[]{:S(2)}) copy-start(bf16[2048]{0:T(1024)(128)(2,1)} %param.14) | copy-start | bytes 12292
  131.5 111.6 %all-gather.6.cloned.1.call-start = ((), (), s32[]{:S(2)}) async-start(), calls=%async_computation.5 | async-start | bytes 1769472 | tf_op jit(solution)/shard_map/all_gather | solution.py:31
  199.7 142.8 %reduce-scatter.6.cloned.1.call-start = ((), (), s32[]{:S(2)}) async-start(), calls=%async_computation.6 | async-start | bytes 11796480 | tf_op jit(solution)/shard_map/reduce_scatter | solution.py:109
  243.1 10.2 %copy-start.2 = (bf16[384,2048]{1,0:T(8,128)(2,1)S(1)}, bf16[384,2048]{1,0:T(8,128)(2,1)}, u32[]{:S(2)}) copy-start(bf16[384,2048]{1,0:T(8,128)(2,1)} %all-gather.6.cloned.1.call-done) | copy-start | bytes 4718596
  266.0 0.7 copy-start.7
  266.0 1.9 copy-start.3
  266.0 103.5 %all-gather.8.cloned.1.call-start = ((), (), s32[]{:S(2)}) async-start(), calls=%async_computation.7 | async-start | bytes 2949120 | tf_op jit(solution)/shard_map/all_gather | solution.py:35
  345.3 99.6 %reduce-scatter.8.cloned.1.call-start = ((), (), s32[]{:S(2)}) async-start(), calls=%async_computation.8 | async-start | bytes 1769472 | tf_op jit(solution)/shard_map/reduce_scatter | solution.py:39
  379.2 65.8 %copy-start = (bf16[48,2048]{1,0:T(8,128)(2,1)S(1)}, bf16[48,2048]{1,0:T(8,128)(2,1)}, u32[]{:S(2)}) copy-start(bf16[48,2048]{1,0:T(8,128)(2,1)} %add_convert_fusion.1) | copy-start | bytes 589828
Sparse Core Ops, SparseCore 0:
  9.5 46.8 all-gather.3
  64.9 47.6 all-reduce.3
  131.6 66.3 reduce-scatter.3
  200.0 43.0 all-gather.5
  266.1 76.2 reduce-scatter.5
  345.5 24.0 all-gather.7
  379.3 65.5 reduce-scatter.7
where the time goes:
time: 454 us; the launch traced here: 453 us
  waiting for transfers between devices  358 us (79%)
  matrix products  44 us (10%)
  blocking collectives  19.3 us (4%)
  other arithmetic  15.3 us (3%)
  between operations  14.3 us (3%)
    reduce_scatter x2, waiting for transfers between devices, row_totals(): lax.psum_scatter(jnp.dot(left_side, weight, preferred_element_type=jnp.fl...  132 us
    all_gather x2, waiting for transfers between devices, gather_rows(): return lax.all_gather(local_part, 'row', axis=0, tiled=True)  91.6 us
    reduce_scatter x1, waiting for transfers between devices, on_device(): lax.psum_scatter(unit_sums, 'col', scatter_dimension=0, tiled=True)  68.4 us
    psum x1, waiting for transfers between devices, on_device(): lax.psum((query_part, pair_part, token_squares), 'col')  41.2 us
    all_gather x1, waiting for transfers between devices, gather_columns(): return lax.all_gather(local_part, 'col', axis=0, tiled=True)  24.2 us
    dot_general x2, matrix products, row_totals(): jnp.dot(left_side, weight, preferred_element_type=jnp.float32)  14.8 us
    dot_general x1, matrix products, on_device(): jnp.dot(unit_input, up_weight, preferred_element_type=jnp.float32)  10.1 us
  transfers between devices with their start and end apart: 7, of which 7 were waited for; matrix products, arithmetic and copies ran while one was open for 1% of the time, Pallas kernels for 0%

commit v1 on v0

v1 whole, which is shorter than its diff:
```python
import functools

import jax
import jax.numpy as jnp
from jax import lax
from jax.experimental import pallas as pl
from jax.experimental.pallas import tpu as pltpu
from jax.sharding import PartitionSpec as P

D = 8192
HEADS = 64
KV_HEADS = 8
HD = 128


rope_base = 500000.0
epsilon = 1e-05


def rotate(values, positions):
    half_width = values.shape[-1] // 2
    frequency = rope_base ** (-(jnp.arange(half_width, dtype=jnp.float32) * 2.0 / values.shape[-1]))
    angles = positions.astype(jnp.float32)[:, None] * frequency[None, :]
    cosine = jnp.cos(angles)[:, None, :]
    sine_part = jnp.sin(angles)[:, None, :]
    first_part = values[..., :half_width]
    second = values[..., half_width:]
    return jnp.concatenate(
        [first_part * cosine - second * sine_part, second * cosine + first_part * sine_part],
        axis=-1,
    )


def remote(axis, source, target, send_sem, recv_sem, device):
    return pltpu.make_async_remote_copy(
        src_ref=source,
        dst_ref=target,
        send_sem=send_sem,
        recv_sem=recv_sem,
        device_id={axis: device},
        device_id_type=pl.DeviceIdType.MESH,
    )


def greet(axis, me, line, depth):
    barrier = pltpu.get_barrier_semaphore()

    def signal(device):
        pl.semaphore_signal(
            barrier, inc=1, device_id={axis: device}, device_id_type=pl.DeviceIdType.MESH
        )

    signal(line * 2 + 1 - me % 2)
    pl.when(line < depth - 1)(lambda: signal(me + 2))
    pl.when(line > 0)(lambda: signal(me - 2))
    inner = (line > 0) & (line < depth - 1)
    pl.when(inner)(lambda: pl.semaphore_wait(barrier, 3))
    pl.when((line == 0) | (line == depth - 1))(lambda: pl.semaphore_wait(barrier, 2))


def gather_kernel(axis, depth, count, *refs):
    own, whole = refs[:count], refs[count : 2 * count]
    up_send, down_send, pair_send, line_recv, pair_recv = refs[2 * count :]
    me = lax.axis_index(axis)
    line, side = me // 2, me % 2
    partner = line * 2 + 1 - side
    greet(axis, me, line, depth)

    def up(k, at, source):
        block = whole[k].at[at * 2 + side]
        return remote(axis, source, block, up_send.at[k, at], line_recv.at[k, at], me + 2)

    def down(k, at, source):
        block = whole[k].at[at * 2 + side]
        return remote(axis, source, block, down_send.at[k, at], line_recv.at[k, at], me - 2)

    def across(k, at, source):
        block = whole[k].at[at * 2 + side]
        return remote(axis, source, block, pair_send.at[k, at], pair_recv.at[k, at], partner)

    for k in range(count):
        pl.when(line < depth - 1)(lambda k=k: up(k, line, own[k]).start())
        pl.when(line > 0)(lambda k=k: down(k, line, own[k]).start())
        across(k, line, own[k]).start()
    for k in range(count):
        whole[k][me] = own[k][...]
    for step in range(1, depth):

        @pl.when(line - step >= 0)
        def _():
            at = line - step
            for k in range(count):
                block = whole[k].at[at * 2 + side]
                remote(
                    axis, block, block, up_send.at[k, at], line_recv.at[k, at], partner
                ).wait_recv()
                pl.when(line < depth - 1)(lambda k=k, block=block: up(k, at, block).start())
                across(k, at, block).start()

        @pl.when(line + step < depth)
        def _():
            at = line + step
            for k in range(count):
                block = whole[k].at[at * 2 + side]
                remote(
                    axis, block, block, down_send.at[k, at], line_recv.at[k, at], partner
                ).wait_recv()
                pl.when(line > 0)(lambda k=k, block=block: down(k, at, block).start())
                across(k, at, block).start()

    for at in range(depth):
        for k in range(count):
            block = whole[k].at[at * 2 + 1 - side]
            sent = whole[k].at[at * 2 + side]
            remote(axis, block, block, pair_send.at[k, at], pair_recv.at[k, at], partner).wait_recv()
            across(k, at, sent).wait_send()
            pl.when((line < depth - 1) & (line >= at))(
                lambda k=k, at=at, sent=sent: up(k, at, sent).wait_send()
            )
            pl.when((line > 0) & (line <= at))(
                lambda k=k, at=at, sent=sent: down(k, at, sent).wait_send()
            )


def scatter_kernel(axis, depth, count, *refs):
    parts, totals = refs[:count], refs[count : 2 * count]
    taken, sums, passed = (refs[(2 + i) * count : (3 + i) * count] for i in range(3))
    pair_send, pair_recv, line_send, line_recv = refs[5 * count :]
    me = lax.axis_index(axis)
    line, side = me // 2, me % 2
    partner = line * 2 + 1 - side
    greet(axis, me, line, depth)

    def across(k, at):
        return remote(
            axis,
            parts[k].at[at * 2 + 1 - side],
            taken[k].at[at],
            pair_send.at[k, at],
            pair_recv.at[k, at],
            partner,
        )

    def along(k, at, slot, device):
        return remote(
            axis,
            sums[k].at[at],
            passed[k].at[slot],
            line_send.at[k, at],
            line_recv.at[k, slot],
            device,
        )

    def add(k, at, slots, target):
        rows = parts[k].shape[1]
        piece = 16 if rows % 16 == 0 else rows

        def body(i, carry):
            here = pl.ds(pl.multiple_of(i * piece, piece), piece)
            value = parts[k][at * 2 + side, here].astype(jnp.float32)
            value = value + taken[k][at, here].astype(jnp.float32)
            for slot in slots:
                value = value + passed[k][slot, here].astype(jnp.float32)
            target[here] = value.astype(target.dtype)
            return carry

        lax.fori_loop(0, rows // piece, body, 0)

    for step in range(depth - 1, 0, -1):

        @pl.when(line + step < depth)
        def _():
            for k in range(count):
                across(k, line + step).start()

        @pl.when(line - step >= 0)
        def _():
            for k in range(count):
                across(k, line - step).start()

    for k in range(count):
        across(k, line).start()

    for step in range(depth - 1, 0, -1):

        @pl.when(line + step < depth)
        def _():
            at = line + step
            for k in range(count):
                across(k, at).wait_recv()

                @pl.when(line > 0)
                def _():
                    along(k, at, at, partner).wait_recv()
                    add(k, at, (at,), sums[k].at[at])

                @pl.when(line == 0)
                def _():
                    add(k, at, (), sums[k].at[at])

                along(k, at, at, me + 2).start()

        @pl.when(line - step >= 0)
        def _():
            at = line - step
            slot = at if step > 1 else depth
            for k in range(count):
                across(k, at).wait_recv()

                @pl.when(line < depth - 1)
                def _():
                    along(k, at, at, partner).wait_recv()
                    add(k, at, (at,), sums[k].at[at])

                @pl.when(line == depth - 1)
                def _():
                    add(k, at, (), sums[k].at[at])

                along(k, at, slot, me - 2).start()

    for k in range(count):
        across(k, line).wait_recv()

        @pl.when(line == 0)
        def _():
            along(k, line, depth, partner).wait_recv()
            add(k, line, (depth,), totals[k])

        @pl.when(line == depth - 1)
        def _():
            along(k, line, line, partner).wait_recv()
            add(k, line, (line,), totals[k])

        @pl.when((line > 0) & (line < depth - 1))
        def _():
            along(k, line, line, partner).wait_recv()
            along(k, line, depth, partner).wait_recv()
            add(k, line, (line, depth), totals[k])

    for at in range(depth):
        for k in range(count):
            across(k, at).wait_send()
            pl.when(line != at)(lambda k=k, at=at: along(k, at, at, partner).wait_send())


def call(kernel, results, arrays, scratch, number):
    in_vmem = pl.BlockSpec(memory_space=pltpu.VMEM)
    return pl.pallas_call(
        kernel,
        out_shape=results,
        in_specs=[in_vmem] * len(arrays),
        out_specs=[in_vmem] * len(results),
        scratch_shapes=scratch,
        compiler_params=pltpu.CompilerParams(collective_id=number, has_side_effects=True),
    )(*arrays)


def gather(axis, number, *arrays):
    size = lax.axis_size(axis)
    depth, count = size // 2, len(arrays)
    semaphores = [pltpu.SemaphoreType.DMA((count, depth))] * 5
    results = [jax.ShapeDtypeStruct((size,) + a.shape, a.dtype) for a in arrays]
    whole = call(
        functools.partial(gather_kernel, axis, depth, count), results, arrays, semaphores, number
    )
    return [w.reshape((size * a.shape[0],) + a.shape[1:]) for w, a in zip(whole, arrays)]


def scatter(axis, number, *arrays):
    size = lax.axis_size(axis)
    depth, count = size // 2, len(arrays)
    parts = [a.reshape((size, a.shape[0] // size) + a.shape[1:]) for a in arrays]
    scratch = [
        pltpu.VMEM((slots,) + p.shape[1:], p.dtype)
        for slots in (depth, depth, depth + 1)
        for p in parts
    ]
    scratch += [pltpu.SemaphoreType.DMA((count, depth))] * 3
    scratch += [pltpu.SemaphoreType.DMA((count, depth + 1))]
    results = [jax.ShapeDtypeStruct(p.shape[1:], jnp.float32) for p in parts]
    return call(
        functools.partial(scatter_kernel, axis, depth, count), results, parts, scratch, number
    )


def product(left_side, weight):
    return jnp.dot(left_side, weight, preferred_element_type=jnp.float32).astype(jnp.bfloat16)


def square_sums(values):
    sums = jnp.sum(values * values, axis=1, keepdims=True)
    return jnp.broadcast_to(sums, (values.shape[0], 128))


def on_device(
    stream,
    attention_gain,
    query_weight,
    pair_weight,
    out_weight,
    unit_gain,
    gate_weight,
    up_weight,
    down_weight,
):
    row_index = lax.axis_index("row")
    column_index = lax.axis_index("col")
    (every_token,) = gather("row", 0, stream)
    tokens = every_token.shape[0]
    query_count = tokens // lax.axis_size("col")
    heads_here = query_weight.shape[1] // HD
    query_width = heads_here * HD
    pair_head = row_index * heads_here // (HEADS // KV_HEADS)
    whole_float = every_token.astype(jnp.float32)
    normed = (whole_float * attention_gain.astype(jnp.float32)).astype(jnp.bfloat16)
    pair_columns = lax.dynamic_slice_in_dim(pair_weight, pair_head * 2 * HD, 2 * HD, 1)
    query_rows, pair_sums, squares = scatter(
        "col",
        1,
        product(normed, query_weight),
        product(normed, pair_columns),
        square_sums(whole_float),
    )
    query_start = column_index * query_count
    row_scale = lax.rsqrt(squares[:, :1] / D + epsilon)
    positions = jnp.arange(tokens, dtype=jnp.int32)
    query_positions = query_start + jnp.arange(query_count, dtype=jnp.int32)
    queries = rotate((row_scale * query_rows).reshape(query_count, heads_here, HD), query_positions)
    pair_values = row_scale * pair_sums
    own_keys = rotate(pair_values[:, :HD].reshape(query_count, 1, HD), query_positions)[:, 0, :]
    own_values = pair_values[:, HD:].astype(jnp.bfloat16)
    key_rows, value_rows = gather("col", 2, own_keys, own_values)
    scores = jnp.einsum("qhd,kd->hqk", queries, key_rows, precision=lax.Precision.HIGHEST) * HD ** (
        -0.5
    )
    causal = query_positions[:, None] >= positions[None, :]
    scores = jnp.where(causal[None, :, :], scores, -1e30)
    largest = jnp.max(scores, axis=-1, keepdims=True)
    exponent = jnp.exp(scores - largest)
    attention = (exponent / jnp.sum(exponent, axis=-1, keepdims=True)).astype(jnp.bfloat16)
    mixture = jnp.einsum("hqk,kd->qhd", attention, value_rows, preferred_element_type=jnp.float32)
    heads_out = mixture.reshape(query_count, query_width).astype(jnp.bfloat16)
    (every_head,) = gather("col", 3, heads_out)
    (attention_rows,) = scatter("row", 4, product(every_head, out_weight))
    hidden_rows = (stream.astype(jnp.float32) + attention_rows).astype(jnp.bfloat16)
    (hidden_all,) = gather("row", 5, hidden_rows)
    hidden_float = hidden_all.astype(jnp.float32)
    unit_input = (hidden_float * unit_gain.astype(jnp.float32)).astype(jnp.bfloat16)
    gate_rows, up_rows, square_rows = scatter(
        "col",
        6,
        product(unit_input, gate_weight),
        product(unit_input, up_weight),
        square_sums(hidden_float),
    )
    unit_scale = lax.rsqrt(square_rows[:, :1] / D + epsilon)
    gate_sums = unit_scale * gate_rows
    upward = unit_scale * up_rows
    (activated,) = gather("col", 7, (jax.nn.silu(gate_sums) * upward).astype(jnp.bfloat16))
    (down_rows,) = scatter("row", 8, product(activated, down_weight))
    return (hidden_rows.astype(jnp.float32) + down_rows).astype(jnp.bfloat16)


def solution(mesh):
    return jax.shard_map(
        on_device,
        mesh=mesh,
        in_specs=(
            P("row", "col"),
            P("col"),
            P("col", "row"),
            P("col", None),
            P("row", "col"),
            P("col"),
            P("col", "row"),
            P("col", "row"),
            P("row", "col"),
        ),
        out_specs=P("row", "col"),
        check_vma=False,
    )
```

time: 454 us -> 255 us (0.56)
  waiting for transfers between devices: 358 us -> 0 us
  Pallas kernels: 0 us -> 185 us
  blocking collectives: 19.3 us -> 0 us
  between operations: 14.3 us -> 0.23 us
    reduce_scatter x3 -> x0, waiting for transfers between devices: 201 us -> none  [the longest x2 132 us: row_totals(): lax.psum_scatter(jnp.dot(left_side, weight, preferred_element_type=jnp.fl...]
    pallas_call x0 -> x9, Pallas kernels: none -> 185 us  [call(): pl.pallas_call(kernel, out_shape=results, in_specs=[in_vmem] * len(arrays...]
    all_gather x3 -> x0, waiting for transfers between devices: 116 us -> none  [the longest x2 91.6 us: gather_rows(): return lax.all_gather(local_part, 'row', axis=0, tiled=True)]
    psum x1 -> x0, waiting for transfers between devices: 41.2 us -> none  [on_device(): lax.psum((query_part, pair_part, token_squares), 'col')]
    all_gather x1 -> x0, blocking collectives: 7.97 us -> none  [gather_columns(): return lax.all_gather(local_part, 'col', axis=0, tiled=True)]
    psum x1 -> x0, blocking collectives: 5.66 us -> none  [on_device(): lax.psum((query_part, pair_part, token_squares), 'col')]
    unnamed x1 -> x0, blocking collectives: 5.66 us -> none
    concatenate x1 -> x0, other arithmetic: 4.69 us -> none  [on_device(): jnp.concatenate([jnp.dot(unit_input, gate_weight, preferred_element_type=...]
  transfers between devices with their start and end apart: 7 -> 0, of which waited for: 7 -> 0; matrix products, arithmetic and copies ran while one was open for 1% -> 0% of each run, Pallas kernels for 0% -> 0%
where the time goes in v1:
time: 255 us; the launch traced here: 254 us
  Pallas kernels  185 us (73%)
  matrix products  46.8 us (18%)
  other arithmetic  18.1 us (7%)
  local copies, waits for them, and re-layouts  3.94 us (2%)
    pallas_call x9, Pallas kernels, call(): pl.pallas_call(kernel, out_shape=results, in_specs=[in_vmem] * len(arrays...  185 us
    dot_general x6, matrix products, product(): jnp.dot(left_side, weight, preferred_element_type=jnp.float32)  44 us

profile of v1, /device:TPU:0, one launch (start us, length us, event | category | flops | bytes accessed | tf_op | source)
XLA Modules:
  0.0 254.2 jit_solution(11103544598471001355)
XLA Ops:
  0.0 0.7 convert_element_type.85
  0.7 0.7 convert_element_type.100
  1.4 0.1 iota_compare_fusion
  1.5 0.2 multiply_cosine_fusion
  1.7 26.7 %shard_map.91 = bf16[8,48,2048]{2,1,0:T(8,128)(2,1)} custom-call(bf16[48,2048]{1,0:T(8,128)(2,1)} %refs_0_.1), custom_call_target="tpu_custom_call" | custom-call | tf_op jit(solution)/shard_map/pallas_call | solution.py:248
  28.5 0.0 copy-start
  28.5 1.9 multiply_reduce_fusion.1
  30.4 0.0 copy-done
  30.4 0.5 fusion.2
  30.9 0.1 broadcast_in_dim.16
  30.9 0.8 broadcast_in_dim.17.refs_2_
  31.7 2.5 convolution_convert_fusion.6
  34.2 4.9 %convolution_convert_fusion.4 = bf16[384,1024]{1,0:T(8,128)(2,1)} fusion(bf16[384,2048]{1,0:T(8,128)(2,1)S(1)} %fusion.2, bf16[2048,1024]{1,0:T(8,128)(2,1)} %param.11), kind=kOutput, calls=%fused_computation.16 | convolution fusion | flops 1611005952 | bytes 6553600 | tf_op jit(solution)/shard_map/dot_general | solution.py:287
  39.1 13.1 %shard_map.92 = (f32[96,1024]{1,0:T(8,128)}, f32[96,256]{1,0:T(8,128)}, f32[96,128]{1,0:T(8,128)}) custom-call(bf16[4,96,1024]{2,1,0:T(8,128)(2,1)} %bitcast.60, bf16[4,96,256]{2,1,0:T(8,128)(2,1)} %bitcast.64, f32[4,96,128]{2,1,0:T(8,128)} %broadcast_in_dim.17.refs_2_), custom_call_target="tpu_custom_call" | custom-call | tf_op jit(solution)/shard_map/pallas_call | solution.py:248
  52.1 0.9 rsqrt_reduce_fusion.1
  53.1 1.0 broadcast_multiply_fusion
  54.0 1.1 multiply_bitcast_fusion
  55.1 0.1 copy.19
  55.2 0.6 slice.47.refs_1_
  55.8 0.3 fusion.16
  56.1 0.7 maximum_bitcast_fusion.refs_0_
  56.8 6.9 %shard_map.93 = (f32[4,96,128]{2,1,0:T(8,128)}, bf16[4,96,128]{2,1,0:T(8,128)(2,1)}) custom-call(f32[96,128]{1,0:T(8,128)} %maximum_bitcast_fusion.refs_0_, bf16[96,128]{1,0:T(8,128)(2,1)} %slice.47.refs_1_), custom_call_target="tpu_custom_call" | custom-call | tf_op jit(solution)/shard_map/pallas_call | solution.py:248
  63.7 0.0 copy-start.4
  63.7 0.2 fusion.22
  63.9 0.1 multiply_subtract_fusion
  64.0 0.6 copy-done.4
  64.6 0.0 copy-start.5
  64.6 1.2 fusion.6
  65.8 0.4 fusion.23
  66.2 0.0 copy-done.5
  66.2 1.6 fusion.7
  67.8 0.7 copy.25
  68.5 10.1 %shard_map.94 = bf16[4,96,1024]{2,1,0:T(8,128)(2,1)} custom-call(bf16[96,1024]{1,0:T(8,128)(2,1)} %bitcast.62), custom_call_target="tpu_custom_call" | custom-call | tf_op jit(solution)/shard_map/pallas_call | solution.py:248
  78.7 5.4 %convolution_convert_fusion.2 = bf16[384,2048]{1,0:T(8,128)(2,1)} fusion(bf16[384,1024]{1,0:T(8,128)(2,1)} %bitcast.61, bf16[1024,2048]{1,0:T(8,128)(2,1)} %param.13), kind=kOutput, calls=%fused_computation.9 | convolution fusion | flops 1611399168 | bytes 6553600 | tf_op jit(solution)/shard_map/dot_general | solution.py:287
  84.0 0.0 copy-start.3
  84.0 24.3 %shard_map.95 = f32[48,2048]{1,0:T(8,128)} custom-call(bf16[8,48,2048]{2,1,0:T(8,128)(2,1)} %bitcast.58), custom_call_target="tpu_custom_call" | custom-call | tf_op jit(solution)/shard_map/pallas_call | solution.py:248
  108.4 0.0 copy-done.3
  108.4 1.7 add_convert_fusion.1.refs_0_
  110.1 24.8 %shard_map.96 = bf16[8,48,2048]{2,1,0:T(8,128)(2,1)} custom-call(bf16[48,2048]{1,0:T(8,128)(2,1)} %add_convert_fusion.1.refs_0_), custom_call_target="tpu_custom_call" | custom-call | tf_op jit(solution)/shard_map/pallas_call | solution.py:248
  134.9 0.0 copy-start.1
  134.9 1.9 multiply_reduce_fusion
  136.8 0.0 copy-done.1
  136.8 0.5 fusion.1
  137.3 0.1 broadcast_in_dim.24
  137.4 0.8 broadcast_in_dim.25.refs_2_
  138.2 10.8 %convolution_convert_fusion = bf16[384,3072]{1,0:T(8,128)(2,1)} fusion(bf16[384,2048]{1,0:T(8,128)(2,1)S(1)} %fusion.1, bf16[2048,3072]{1,0:T(8,128)(2,1)} %param.16), kind=kOutput, calls=%fused_computation.1 | convolution fusion | flops 4833017856 | bytes 16515072 | tf_op jit(solution)/shard_map/dot_general | solution.py:287
  149.0 10.9 %convolution_convert_fusion.1 = bf16[384,3072]{1,0:T(8,128)(2,1)} fusion(bf16[384,2048]{1,0:T(8,128)(2,1)S(1)} %fusion.1, bf16[2048,3072]{1,0:T(8,128)(2,1)} %param.15), kind=kOutput, calls=%fused_computation.2 | convolution fusion | flops 4833017856 | bytes 16515072 | tf_op jit(solution)/shard_map/dot_general | solution.py:287
  159.8 34.1 %shard_map.97 = (f32[96,3072]{1,0:T(8,128)}, f32[96,3072]{1,0:T(8,128)}, f32[96,128]{1,0:T(8,128)}) custom-call(bf16[4,96,3072]{2,1,0:T(8,128)(2,1)} %bitcast.56, bf16[4,96,3072]{2,1,0:T(8,128)(2,1)} %bitcast.55, f32[4,96,128]{2,1,0:T(8,128)} %broadcast_in_dim.25.refs_2_), custom_call_target="tpu_custom_call" | custom-call | tf_op jit(solution)/shard_map/pallas_call | solution.py:248
  193.9 0.9 rsqrt_reduce_fusion
  194.9 2.9 %multiply_convert_fusion.refs_0_ = bf16[96,3072]{1,0:T(8,128)(2,1)} fusion(f32[96,3072]{1,0:T(8,128)} %get-tuple-element.20, f32[96,3072]{1,0:T(8,128)} %get-tuple-element.19, f32[96]{0:T(128)S(1)} %rsqrt_reduce_fusion), kind=kLoop, calls=%fused_computation.17 | loop fusion | flops 2359296 | bytes 2949504 | tf_op jit(solution)/shard_map/convert_element_type | solution.py:359
  197.7 20.2 %shard_map.98 = bf16[4,96,3072]{2,1,0:T(8,128)(2,1)} custom-call(bf16[96,3072]{1,0:T(8,128)(2,1)} %multiply_convert_fusion.refs_0_), custom_call_target="tpu_custom_call" | custom-call | tf_op jit(solution)/shard_map/pallas_call | solution.py:248
  218.0 9.7 %convolution_convert_fusion.3 = bf16[384,2048]{1,0:T(8,128)(2,1)} fusion(bf16[384,3072]{1,0:T(8,128)(2,1)} %bitcast.57, bf16[3072,2048]{1,0:T(8,128)(2,1)} %param.17), kind=kOutput, calls=%fused_computation.10 | convolution fusion | flops 4832624640 | bytes 16515072 | tf_op jit(solution)/shard_map/dot_general | solution.py:287
  227.6 0.0 copy-start.2
  227.6 24.8 %shard_map.99 = f32[48,2048]{1,0:T(8,128)} custom-call(bf16[8,48,2048]{2,1,0:T(8,128)(2,1)} %bitcast.59), custom_call_target="tpu_custom_call" | custom-call | tf_op jit(solution)/shard_map/pallas_call | solution.py:248
  252.4 0.0 copy-done.2
  252.5 1.7 add_convert_fusion
  (3 shorter events, 0.0 us)
Async XLA Ops:
  28.5 1.9 copy-start
  63.7 0.9 copy-start.4
  64.6 1.6 copy-start.5
  84.0 24.4 %copy-start.3 = (bf16[48,2048]{1,0:T(8,128)(2,1)S(1)}, bf16[48,2048]{1,0:T(8,128)(2,1)}, u32[]{:S(2)}) copy-start(bf16[48,2048]{1,0:T(8,128)(2,1)} %refs_0_.1) | copy-start | bytes 589828
  134.9 1.9 copy-start.1
  227.6 24.8 %copy-start.2 = (bf16[48,2048]{1,0:T(8,128)(2,1)S(1)}, bf16[48,2048]{1,0:T(8,128)(2,1)}, u32[]{:S(2)}) copy-start(bf16[48,2048]{1,0:T(8,128)(2,1)} %add_convert_fusion.1.refs_0_) | copy-start | bytes 589828

commit v2 on v1

--- a/solution.py
+++ b/solution.py
@@ -58,9 +58,28 @@
     pl.when((line == 0) | (line == depth - 1))(lambda: pl.semaphore_wait(barrier, 2))
 
 
-def gather_kernel(axis, depth, count, *refs):
-    own, whole = refs[:count], refs[count : 2 * count]
+def cut(shape, dtype):
+    rows, most = shape[0] // 16, shape[0] * shape[1] * jnp.dtype(dtype).itemsize // 49152
+    if shape[0] % 16:
+        return 1
+    return max(p for p in range(1, rows + 1) if rows % p == 0 and p <= max(most, 1))
+
+
+def views(refs, pieces):
+    return [
+        ref.at[:, pl.ds(i * (ref.shape[1] // runs), ref.shape[1] // runs)]
+        for ref, runs in zip(refs, pieces)
+        for i in range(runs)
+    ]
+
+
+def gather_kernel(axis, depth, pieces, *refs):
+    count = len(pieces)
+    kept, full = refs[:count], refs[count : 2 * count]
     up_send, down_send, pair_send, line_recv, pair_recv = refs[2 * count :]
+    own = [view.at[0] for view in views(kept, pieces)]
+    whole = views(full, pieces)
+    count = len(whole)
     me = lax.axis_index(axis)
     line, side = me // 2, me % 2
     partner = line * 2 + 1 - side
@@ -82,31 +101,20 @@
         pl.when(line < depth - 1)(lambda k=k: up(k, line, own[k]).start())
         pl.when(line > 0)(lambda k=k: down(k, line, own[k]).start())
         across(k, line, own[k]).start()
-    for k in range(count):
-        whole[k][me] = own[k][...]
+    for source, target in zip(kept, full):
+        target[me] = source[0]
+    def pass_on(k, at, more, send):
+        block = whole[k].at[at * 2 + side]
+        remote(
+            axis, block, block, pair_send.at[k, at], line_recv.at[k, at], partner
+        ).wait_recv()
+        pl.when(more)(lambda: send(k, at, block).start())
+        across(k, at, block).start()
+
     for step in range(1, depth):
-
-        @pl.when(line - step >= 0)
-        def _():
-            at = line - step
-            for k in range(count):
-                block = whole[k].at[at * 2 + side]
-                remote(
-                    axis, block, block, up_send.at[k, at], line_recv.at[k, at], partner
-                ).wait_recv()
-                pl.when(line < depth - 1)(lambda k=k, block=block: up(k, at, block).start())
-                across(k, at, block).start()
-
-        @pl.when(line + step < depth)
-        def _():
-            at = line + step
-            for k in range(count):
-                block = whole[k].at[at * 2 + side]
-                remote(
-                    axis, block, block, down_send.at[k, at], line_recv.at[k, at], partner
-                ).wait_recv()
-                pl.when(line > 0)(lambda k=k, block=block: down(k, at, block).start())
-                across(k, at, block).start()
+        for k in range(count):
+            pl.when(line - step >= 0)(lambda: pass_on(k, line - step, line < depth - 1, up))
+            pl.when(line + step < depth)(lambda: pass_on(k, line + step, line > 0, down))
 
     for at in range(depth):
         for k in range(count):
@@ -122,10 +130,13 @@
             )
 
 
-def scatter_kernel(axis, depth, count, *refs):
-    parts, totals = refs[:count], refs[count : 2 * count]
-    taken, sums, passed = (refs[(2 + i) * count : (3 + i) * count] for i in range(3))
+def scatter_kernel(axis, depth, pieces, *refs):
+    count = len(pieces)
+    parts, totals, taken, sums, passed = (
+        views(refs[i * count : (i + 1) * count], pieces) for i in range(5)
+    )
     pair_send, pair_recv, line_send, line_recv = refs[5 * count :]
+    count = len(parts)
     me = lax.axis_index(axis)
     line, side = me // 2, me % 2
     partner = line * 2 + 1 - side
@@ -152,7 +163,7 @@
         )
 
     def add(k, at, slots, target):
-        rows = parts[k].shape[1]
+        rows = target.shape[0]
         piece = 16 if rows % 16 == 0 else rows
 
         def body(i, carry):
@@ -167,56 +178,38 @@
         lax.fori_loop(0, rows // piece, body, 0)
 
     for step in range(depth - 1, 0, -1):
-
-        @pl.when(line + step < depth)
-        def _():
-            for k in range(count):
-                across(k, line + step).start()
-
-        @pl.when(line - step >= 0)
-        def _():
-            for k in range(count):
-                across(k, line - step).start()
+        for k in range(count):
+            pl.when(line + step < depth)(lambda: across(k, line + step).start())
+            pl.when(line - step >= 0)(lambda: across(k, line - step).start())
 
     for k in range(count):
         across(k, line).start()
 
+    def pass_on(k, at, first, slot, device):
+        across(k, at).wait_recv()
+
+        @pl.when(jnp.logical_not(first))
+        def _():
+            along(k, at, at, partner).wait_recv()
+            add(k, at, (at,), sums[k].at[at])
+
+        @pl.when(first)
+        def _():
+            add(k, at, (), sums[k].at[at])
+
+        along(k, at, slot, device).start()
+
     for step in range(depth - 1, 0, -1):
-
-        @pl.when(line + step < depth)
-        def _():
-            at = line + step
-            for k in range(count):
-                across(k, at).wait_recv()
-
-                @pl.when(line > 0)
-                def _():
-                    along(k, at, at, partner).wait_recv()
-                    add(k, at, (at,), sums[k].at[at])
-
-                @pl.when(line == 0)
-                def _():
-                    add(k, at, (), sums[k].at[at])
-
-                along(k, at, at, me + 2).start()
-
-        @pl.when(line - step >= 0)
-        def _():
-            at = line - step
-            slot = at if step > 1 else depth
-            for k in range(count):
-                across(k, at).wait_recv()
-
-                @pl.when(line < depth - 1)
-                def _():
-                    along(k, at, at, partner).wait_recv()
-                    add(k, at, (at,), sums[k].at[at])
-
-                @pl.when(line == depth - 1)
-                def _():
-                    add(k, at, (), sums[k].at[at])
-
-                along(k, at, slot, me - 2).start()
+        for k in range(count):
+
+            @pl.when(line + step < depth)
+            def _():
+                pass_on(k, line + step, line == 0, line + step, me + 2)
+
+            @pl.when(line - step >= 0)
+            def _():
+                slot = line - step if step > 1 else depth
+                pass_on(k, line - step, line == depth - 1, slot, me - 2)
 
     for k in range(count):
         across(k, line).wait_recv()
@@ -224,18 +217,18 @@
         @pl.when(line == 0)
         def _():
             along(k, line, depth, partner).wait_recv()
-            add(k, line, (depth,), totals[k])
+            add(k, line, (depth,), totals[k].at[0])
 
         @pl.when(line == depth - 1)
         def _():
             along(k, line, line, partner).wait_recv()
-            add(k, line, (line,), totals[k])
+            add(k, line, (line,), totals[k].at[0])
 
         @pl.when((line > 0) & (line < depth - 1))
         def _():
             along(k, line, line, partner).wait_recv()
             along(k, line, depth, partner).wait_recv()
-            add(k, line, (line, depth), totals[k])
+            add(k, line, (line, depth), totals[k].at[0])
 
     for at in range(depth):
         for k in range(count):
@@ -257,19 +250,25 @@
 
 def gather(axis, number, *arrays):
     size = lax.axis_size(axis)
-    depth, count = size // 2, len(arrays)
-    semaphores = [pltpu.SemaphoreType.DMA((count, depth))] * 5
+    depth, pieces = size // 2, [cut(a.shape, a.dtype) for a in arrays]
+    semaphores = [pltpu.SemaphoreType.DMA((sum(pieces), depth))] * 5
     results = [jax.ShapeDtypeStruct((size,) + a.shape, a.dtype) for a in arrays]
     whole = call(
-        functools.partial(gather_kernel, axis, depth, count), results, arrays, semaphores, number
+        functools.partial(gather_kernel, axis, depth, pieces),
+        results,
+        [a[None] for a in arrays],
+        semaphores,
+        number,
     )
     return [w.reshape((size * a.shape[0],) + a.shape[1:]) for w, a in zip(whole, arrays)]
 
 
 def scatter(axis, number, *arrays):
     size = lax.axis_size(axis)
-    depth, count = size // 2, len(arrays)
+    depth = size // 2
     parts = [a.reshape((size, a.shape[0] // size) + a.shape[1:]) for a in arrays]
+    pieces = [cut(p.shape[1:], p.dtype) for p in parts]
+    count = sum(pieces)
     scratch = [
         pltpu.VMEM((slots,) + p.shape[1:], p.dtype)
         for slots in (depth, depth, depth + 1)
@@ -277,10 +276,11 @@
     ]
     scratch += [pltpu.SemaphoreType.DMA((count, depth))] * 3
     scratch += [pltpu.SemaphoreType.DMA((count, depth + 1))]
-    results = [jax.ShapeDtypeStruct(p.shape[1:], jnp.float32) for p in parts]
-    return call(
-        functools.partial(scatter_kernel, axis, depth, count), results, parts, scratch, number
-    )
+    results = [jax.ShapeDtypeStruct((1,) + p.shape[1:], jnp.float32) for p in parts]
+    sums = call(
+        functools.partial(scatter_kernel, axis, depth, pieces), results, parts, scratch, number
+    )
+    return [s[0] for s in sums]
 
 
 def product(left_side, weight):

time: 255 us -> 246 us (0.965)
  Pallas kernels: 185 us -> 176 us
    pallas_call x9, Pallas kernels: 185 us -> 176 us  [call(): pl.pallas_call(kernel, out_shape=results, in_specs=[in_vmem] * len(arrays...]
where the time goes in v2:
time: 246 us; the launch traced here: 245 us
  Pallas kernels  176 us (72%)
  matrix products  46.8 us (19%)
  other arithmetic  17.2 us (7%)
  local copies, waits for them, and re-layouts  4.33 us (2%)
    pallas_call x9, Pallas kernels, call(): pl.pallas_call(kernel, out_shape=results, in_specs=[in_vmem] * len(arrays...  176 us
    dot_general x6, matrix products, product(): jnp.dot(left_side, weight, preferred_element_type=jnp.float32)  44 us

profile of v2, /device:TPU:0, one launch (start us, length us, event | category | flops | bytes accessed | tf_op | source)
XLA Modules:
  0.0 245.0 jit_solution(4599924296880195755)
XLA Ops:
  0.0 0.7 convert_element_type.95
  0.7 0.7 convert_element_type.110
  1.4 0.1 iota_compare_fusion
  1.5 0.2 multiply_cosine_fusion
  1.7 24.4 %shard_map.91 = bf16[8,48,2048]{2,1,0:T(8,128)(2,1)} custom-call(bf16[1,48,2048]{2,1,0:T(8,128)(2,1)} %bitcast.74), custom_call_target="tpu_custom_call" | custom-call | tf_op jit(solution)/shard_map/pallas_call | solution.py:241
  26.2 0.0 copy-start.1
  26.2 1.9 multiply_reduce_fusion.1
  28.1 0.0 copy-done.1
  28.1 0.5 fusion.2
  28.6 0.1 broadcast_in_dim.27
  28.7 0.8 broadcast_in_dim.28.refs_2_
  29.5 2.5 %convolution_convert_fusion.6 = bf16[384,256]{1,0:T(8,128)(2,1)} fusion(bf16[384,2048]{1,0:T(8,128)(2,1)S(1)} %fusion.2, bf16[2048,2048]{1,0:T(8,128)(2,1)} %param.12, s32[]{:T(128)S(6)} %select_n.13), kind=kOutput, calls=%fused_computation.20 | convolution fusion | flops 402751488 | bytes 2818052 | tf_op jit(solution)/shard_map/dot_general | solution.py:287
  31.9 4.9 %convolution_convert_fusion.4 = bf16[384,1024]{1,0:T(8,128)(2,1)} fusion(bf16[384,2048]{1,0:T(8,128)(2,1)S(1)} %fusion.2, bf16[2048,1024]{1,0:T(8,128)(2,1)} %param.11), kind=kOutput, calls=%fused_computation.16 | convolution fusion | flops 1611005952 | bytes 6553600 | tf_op jit(solution)/shard_map/dot_general | solution.py:287
  36.8 13.0 %shard_map.92 = (f32[1,96,1024]{2,1,0:T(8,128)}, f32[1,96,256]{2,1,0:T(8,128)}, f32[1,96,128]{2,1,0:T(8,128)}) custom-call(bf16[4,96,1024]{2,1,0:T(8,128)(2,1)} %bitcast.78, bf16[4,96,256]{2,1,0:T(8,128)(2,1)} %bitcast.82, f32[4,96,128]{2,1,0:T(8,128)} %broadcast_in_dim.28.refs_2_), custom_call_target="tpu_custom_call" | custom-call | tf_op jit(solution)/shard_map/pallas_call | solution.py:241
  49.8 0.9 fusion.25
  50.7 1.0 bitcast_multiply_fusion.2
  51.7 0.6 fusion.26.refs_1_
  52.3 0.3 fusion.18
  52.6 0.7 maximum_bitcast_fusion.refs_0_
  53.3 6.9 %shard_map.93 = (f32[4,96,128]{2,1,0:T(8,128)}, bf16[4,96,128]{2,1,0:T(8,128)(2,1)}) custom-call(f32[1,96,128]{2,1,0:T(8,128)} %maximum_bitcast_fusion.refs_0_, bf16[1,96,128]{2,1,0:T(8,128)(2,1)} %fusion.26.refs_1_), custom_call_target="tpu_custom_call" | custom-call | tf_op jit(solution)/shard_map/pallas_call | solution.py:241
  60.2 0.0 copy-start.4
  60.2 1.1 copy.14
  61.3 0.1 copy_multiply_fusion
  61.4 0.2 multiply_subtract_fusion
  61.6 0.0 copy-done.4
  61.7 0.0 copy-start.5
  61.7 1.2 fusion.6
  62.9 0.4 fusion.32
  63.2 0.0 copy-done.5
  63.3 1.6 fusion.7
  64.8 0.1 copy.13
  64.9 0.8 convert_element_type.104.refs_0_
  65.7 10.1 %shard_map.94 = bf16[4,96,1024]{2,1,0:T(8,128)(2,1)} custom-call(bf16[1,96,1024]{2,1,0:T(8,128)(2,1)} %convert_element_type.104.refs_0_), custom_call_target="tpu_custom_call" | custom-call | tf_op jit(solution)/shard_map/pallas_call | solution.py:241
  75.8 5.4 %convolution_convert_fusion.2 = bf16[384,2048]{1,0:T(8,128)(2,1)} fusion(bf16[384,1024]{1,0:T(8,128)(2,1)} %bitcast.79, bf16[1024,2048]{1,0:T(8,128)(2,1)} %param.13), kind=kOutput, calls=%fused_computation.9 | convolution fusion | flops 1611399168 | bytes 6553600 | tf_op jit(solution)/shard_map/dot_general | solution.py:287
  81.2 0.0 copy-start.3
  81.2 22.9 %shard_map.95 = f32[1,48,2048]{2,1,0:T(8,128)} custom-call(bf16[8,48,2048]{2,1,0:T(8,128)(2,1)} %bitcast.76), custom_call_target="tpu_custom_call" | custom-call | tf_op jit(solution)/shard_map/pallas_call | solution.py:241
  104.1 0.0 copy-done.3
  104.1 1.7 fusion.31.refs_0_
  105.9 22.3 %shard_map.96 = bf16[8,48,2048]{2,1,0:T(8,128)(2,1)} custom-call(bf16[1,48,2048]{2,1,0:T(8,128)(2,1)} %fusion.31.refs_0_), custom_call_target="tpu_custom_call" | custom-call | tf_op jit(solution)/shard_map/pallas_call | solution.py:241
  128.2 0.0 copy-start
  128.2 1.9 multiply_reduce_fusion
  130.1 0.0 copy-done
  130.1 0.5 fusion.1
  130.6 0.1 broadcast_in_dim.33
  130.7 0.8 broadcast_in_dim.34.refs_2_
  131.5 10.8 %convolution_convert_fusion = bf16[384,3072]{1,0:T(8,128)(2,1)} fusion(bf16[384,2048]{1,0:T(8,128)(2,1)S(1)} %fusion.1, bf16[2048,3072]{1,0:T(8,128)(2,1)} %param.16), kind=kOutput, calls=%fused_computation.1 | convolution fusion | flops 4833017856 | bytes 16515072 | tf_op jit(solution)/shard_map/dot_general | solution.py:287
  142.3 10.9 %convolution_convert_fusion.1 = bf16[384,3072]{1,0:T(8,128)(2,1)} fusion(bf16[384,2048]{1,0:T(8,128)(2,1)S(1)} %fusion.1, bf16[2048,3072]{1,0:T(8,128)(2,1)} %param.15), kind=kOutput, calls=%fused_computation.2 | convolution fusion | flops 4833017856 | bytes 16515072 | tf_op jit(solution)/shard_map/dot_general | solution.py:287
  153.1 34.5 %shard_map.97 = (f32[1,96,3072]{2,1,0:T(8,128)}, f32[1,96,3072]{2,1,0:T(8,128)}, f32[1,96,128]{2,1,0:T(8,128)}) custom-call(bf16[4,96,3072]{2,1,0:T(8,128)(2,1)} %bitcast.72, bf16[4,96,3072]{2,1,0:T(8,128)(2,1)} %bitcast.71, f32[4,96,128]{2,1,0:T(8,128)} %broadcast_in_dim.34.refs_2_), custom_call_target="tpu_custom_call" | custom-call | tf_op jit(solution)/shard_map/pallas_call | solution.py:241
  187.6 0.9 fusion.22
  188.5 2.9 %multiply_convert_fusion.refs_0_ = bf16[1,96,3072]{2,1,0:T(8,128)(2,1)} fusion(f32[1,96,3072]{2,1,0:T(8,128)} %get-tuple-element.20, f32[1,96,3072]{2,1,0:T(8,128)} %get-tuple-element.19, f32[96]{0:T(128)S(1)} %fusion.22), kind=kLoop, calls=%fused_computation.17 | loop fusion | flops 2359296 | bytes 2949504 | tf_op jit(solution)/shard_map/convert_element_type | solution.py:359
  191.4 19.7 %shard_map.98 = bf16[4,96,3072]{2,1,0:T(8,128)(2,1)} custom-call(bf16[1,96,3072]{2,1,0:T(8,128)(2,1)} %multiply_convert_fusion.refs_0_), custom_call_target="tpu_custom_call" | custom-call | tf_op jit(solution)/shard_map/pallas_call | solution.py:241
  211.0 9.7 %convolution_convert_fusion.3 = bf16[384,2048]{1,0:T(8,128)(2,1)} fusion(bf16[384,3072]{1,0:T(8,128)(2,1)} %bitcast.73, bf16[3072,2048]{1,0:T(8,128)(2,1)} %param.17), kind=kOutput, calls=%fused_computation.10 | convolution fusion | flops 4832624640 | bytes 16515072 | tf_op jit(solution)/shard_map/dot_general | solution.py:287
  220.7 0.0 copy-start.2
  220.7 22.5 %shard_map.99 = f32[1,48,2048]{2,1,0:T(8,128)} custom-call(bf16[8,48,2048]{2,1,0:T(8,128)(2,1)} %bitcast.77), custom_call_target="tpu_custom_call" | custom-call | tf_op jit(solution)/shard_map/pallas_call | solution.py:241
  243.2 0.0 copy-done.2
  243.2 1.7 fusion.12
  (3 shorter events, 0.0 us)
Async XLA Ops:
  26.2 1.9 copy-start.1
  60.2 1.5 copy-start.4
  61.7 1.6 copy-start.5
  81.2 22.9 %copy-start.3 = (bf16[48,2048]{1,0:T(8,128)(2,1)S(1)}, bf16[48,2048]{1,0:T(8,128)(2,1)}, u32[]{:S(2)}) copy-start(bf16[48,2048]{1,0:T(8,128)(2,1)} %param.9) | copy-start | bytes 589828
  128.2 1.9 copy-start
  220.7 22.5 %copy-start.2 = (f32[1,48,2048]{2,1,0:T(8,128)S(1)}, f32[1,48,2048]{2,1,0:T(8,128)}, u32[]{:S(2)}) copy-start(f32[1,48,2048]{2,1,0:T(8,128)} %shard_map.95) | copy-start | bytes 1179652

commit v3 on v2

--- a/solution.py
+++ b/solution.py
@@ -130,12 +130,31 @@
             )
 
 
-def scatter_kernel(axis, depth, pieces, *refs):
+def multiply(left, weight, made):
+    size, rows, width = made.shape
+    tile = 256 if width % 256 == 0 else width
+
+    def body(i, carry):
+        columns = pl.ds(pl.multiple_of(i * tile, tile), tile)
+        value = jnp.dot(left[...], weight[:, columns], preferred_element_type=jnp.float32)
+        for b in range(size):
+            made[b, :, columns] = value[b * rows : (b + 1) * rows].astype(made.dtype)
+        return carry
+
+    lax.fori_loop(0, width // tile, body, 0)
+
+
+def scatter_kernel(axis, depth, pieces, late, *refs):
     count = len(pieces)
-    parts, totals, taken, sums, passed = (
-        views(refs[i * count : (i + 1) * count], pieces) for i in range(5)
-    )
-    pair_send, pair_recv, line_send, line_recv = refs[5 * count :]
+    given, refs = refs[: count - late], refs[count - late :]
+    operands, refs = refs[: 2 * late], refs[2 * late :]
+    results, refs = refs[:count], refs[count:]
+    made, refs = refs[:late], refs[late:]
+    parts, totals = views(given + made, pieces), views(results, pieces)
+    taken, sums, passed = (
+        views(refs[i * count : (i + 1) * count], pieces) for i in range(3)
+    )
+    pair_send, pair_recv, line_send, line_recv = refs[3 * count :]
     count = len(parts)
     me = lax.axis_index(axis)
     line, side = me // 2, me % 2
@@ -177,14 +196,6 @@
 
         lax.fori_loop(0, rows // piece, body, 0)
 
-    for step in range(depth - 1, 0, -1):
-        for k in range(count):
-            pl.when(line + step < depth)(lambda: across(k, line + step).start())
-            pl.when(line - step >= 0)(lambda: across(k, line - step).start())
-
-    for k in range(count):
-        across(k, line).start()
-
     def pass_on(k, at, first, slot, device):
         across(k, at).wait_recv()
 
@@ -199,17 +210,30 @@
 
         along(k, at, slot, device).start()
 
-    for step in range(depth - 1, 0, -1):
-        for k in range(count):
-
-            @pl.when(line + step < depth)
-            def _():
-                pass_on(k, line + step, line == 0, line + step, me + 2)
-
-            @pl.when(line - step >= 0)
-            def _():
-                slot = line - step if step > 1 else depth
-                pass_on(k, line - step, line == depth - 1, slot, me - 2)
+    def travel(turns):
+        for step in range(depth - 1, 0, -1):
+            for k in turns:
+                pl.when(line + step < depth)(lambda: across(k, line + step).start())
+                pl.when(line - step >= 0)(lambda: across(k, line - step).start())
+        for k in turns:
+            across(k, line).start()
+        for step in range(depth - 1, 0, -1):
+            for k in turns:
+
+                @pl.when(line + step < depth)
+                def _():
+                    pass_on(k, line + step, line == 0, line + step, me + 2)
+
+                @pl.when(line - step >= 0)
+                def _():
+                    slot = line - step if step > 1 else depth
+                    pass_on(k, line - step, line == depth - 1, slot, me - 2)
+
+    ready = count - pieces[-1] if late else count
+    travel(range(ready))
+    if late:
+        multiply(*operands, *made)
+        travel(range(ready, count))
 
     for k in range(count):
         across(k, line).wait_recv()
@@ -263,22 +287,31 @@
     return [w.reshape((size * a.shape[0],) + a.shape[1:]) for w, a in zip(whole, arrays)]
 
 
-def scatter(axis, number, *arrays):
+def scatter(axis, number, *arrays, late=()):
     size = lax.axis_size(axis)
     depth = size // 2
     parts = [a.reshape((size, a.shape[0] // size) + a.shape[1:]) for a in arrays]
-    pieces = [cut(p.shape[1:], p.dtype) for p in parts]
+    blocks = [jax.ShapeDtypeStruct(p.shape, p.dtype) for p in parts]
+    if late:
+        shape = (size, late[0].shape[0] // size, late[1].shape[1])
+        blocks.append(jax.ShapeDtypeStruct(shape, jnp.bfloat16))
+    pieces = [cut(p.shape[1:], p.dtype) for p in blocks]
     count = sum(pieces)
-    scratch = [
+    scratch = [pltpu.VMEM(shape, jnp.bfloat16)] if late else []
+    scratch += [
         pltpu.VMEM((slots,) + p.shape[1:], p.dtype)
         for slots in (depth, depth, depth + 1)
-        for p in parts
+        for p in blocks
     ]
     scratch += [pltpu.SemaphoreType.DMA((count, depth))] * 3
     scratch += [pltpu.SemaphoreType.DMA((count, depth + 1))]
-    results = [jax.ShapeDtypeStruct((1,) + p.shape[1:], jnp.float32) for p in parts]
+    results = [jax.ShapeDtypeStruct((1,) + p.shape[1:], jnp.float32) for p in blocks]
     sums = call(
-        functools.partial(scatter_kernel, axis, depth, pieces), results, parts, scratch, number
+        functools.partial(scatter_kernel, axis, depth, pieces, len(late) // 2),
+        results,
+        [*parts, *late],
+        scratch,
+        number,
     )
     return [s[0] for s in sums]
 
@@ -346,12 +379,12 @@
     (hidden_all,) = gather("row", 5, hidden_rows)
     hidden_float = hidden_all.astype(jnp.float32)
     unit_input = (hidden_float * unit_gain.astype(jnp.float32)).astype(jnp.bfloat16)
-    gate_rows, up_rows, square_rows = scatter(
+    gate_rows, square_rows, up_rows = scatter(
         "col",
         6,
         product(unit_input, gate_weight),
-        product(unit_input, up_weight),
         square_sums(hidden_float),
+        late=(unit_input, up_weight),
     )
     unit_scale = lax.rsqrt(square_rows[:, :1] / D + epsilon)
     gate_sums = unit_scale * gate_rows

time: 246 us -> 239 us (0.972)
  matrix products: 46.8 us -> 36 us
  Pallas kernels: 176 us -> 180 us
    dot_general x6 -> x5, matrix products: 44 us -> 33.2 us  [product(): jnp.dot(left_side, weight, preferred_element_type=jnp.float32)]
    pallas_call x9, Pallas kernels: 176 us -> 180 us  [call(): pl.pallas_call(kernel, out_shape=results, in_specs=[in_vmem] * len(arrays...]
where the time goes in v3:
time: 239 us; the launch traced here: 238 us
  Pallas kernels  180 us (75%)
  matrix products  36 us (15%)
  other arithmetic  17.2 us (7%)
  local copies, waits for them, and re-layouts  4.52 us (2%)
    pallas_call x9, Pallas kernels, call(): pl.pallas_call(kernel, out_shape=results, in_specs=[in_vmem] * len(arrays...  180 us
    dot_general x5, matrix products, product(): jnp.dot(left_side, weight, preferred_element_type=jnp.float32)  33.2 us

profile of v3, /device:TPU:0, one launch (start us, length us, event | category | flops | bytes accessed | tf_op | source)
XLA Modules:
  0.0 237.8 jit_solution(2204919284404364250)
XLA Ops:
  0.0 0.7 convert_element_type.92
  0.7 0.7 convert_element_type.107
  1.4 0.1 iota_compare_fusion
  1.5 0.2 multiply_cosine_fusion
  1.7 24.4 %shard_map.91 = bf16[8,48,2048]{2,1,0:T(8,128)(2,1)} custom-call(bf16[1,48,2048]{2,1,0:T(8,128)(2,1)} %bitcast.70), custom_call_target="tpu_custom_call" | custom-call | tf_op jit(solution)/shard_map/pallas_call | solution.py:265
  26.2 0.0 copy-start.1
  26.2 1.9 multiply_reduce_fusion.1
  28.1 0.0 copy-done.1
  28.1 0.5 fusion.2
  28.6 0.1 broadcast_in_dim.27
  28.7 0.8 broadcast_in_dim.28.refs_2_
  29.5 2.5 %convolution_convert_fusion.5 = bf16[384,256]{1,0:T(8,128)(2,1)} fusion(bf16[384,2048]{1,0:T(8,128)(2,1)S(1)} %fusion.2, bf16[2048,2048]{1,0:T(8,128)(2,1)} %param.12, s32[]{:T(128)S(6)} %select_n.13), kind=kOutput, calls=%fused_computation.19 | convolution fusion | flops 402751488 | bytes 2818052 | tf_op jit(solution)/shard_map/dot_general | solution.py:320
  31.9 4.9 %convolution_convert_fusion.3 = bf16[384,1024]{1,0:T(8,128)(2,1)} fusion(bf16[384,2048]{1,0:T(8,128)(2,1)S(1)} %fusion.2, bf16[2048,1024]{1,0:T(8,128)(2,1)} %param.11), kind=kOutput, calls=%fused_computation.15 | convolution fusion | flops 1611005952 | bytes 6553600 | tf_op jit(solution)/shard_map/dot_general | solution.py:320
  36.8 13.0 %shard_map.92 = (f32[1,96,1024]{2,1,0:T(8,128)}, f32[1,96,256]{2,1,0:T(8,128)}, f32[1,96,128]{2,1,0:T(8,128)}) custom-call(bf16[4,96,1024]{2,1,0:T(8,128)(2,1)} %bitcast.74, bf16[4,96,256]{2,1,0:T(8,128)(2,1)} %bitcast.78, f32[4,96,128]{2,1,0:T(8,128)} %broadcast_in_dim.28.refs_2_), custom_call_target="tpu_custom_call" | custom-call | tf_op jit(solution)/shard_map/pallas_call | solution.py:265
  49.8 0.9 fusion.25
  50.7 1.0 bitcast_multiply_fusion.2
  51.7 0.6 fusion.26.refs_1_
  52.3 0.3 fusion.18
  52.6 0.7 maximum_bitcast_fusion.refs_0_
  53.3 6.9 %shard_map.93 = (f32[4,96,128]{2,1,0:T(8,128)}, bf16[4,96,128]{2,1,0:T(8,128)(2,1)}) custom-call(f32[1,96,128]{2,1,0:T(8,128)} %maximum_bitcast_fusion.refs_0_, bf16[1,96,128]{2,1,0:T(8,128)(2,1)} %fusion.26.refs_1_), custom_call_target="tpu_custom_call" | custom-call | tf_op jit(solution)/shard_map/pallas_call | solution.py:265
  60.2 0.0 copy-start.5
  60.2 1.1 copy.14
  61.3 0.1 copy_multiply_fusion
  61.4 0.2 multiply_subtract_fusion
  61.6 0.0 copy-done.5
  61.7 0.0 copy-start.6
  61.7 1.2 fusion.6
  62.9 0.4 fusion.32
  63.2 0.0 copy-done.6
  63.3 1.6 fusion.7
  64.8 0.1 copy.13
  64.9 0.8 convert_element_type.101.refs_0_
  65.7 10.1 %shard_map.94 = bf16[4,96,1024]{2,1,0:T(8,128)(2,1)} custom-call(bf16[1,96,1024]{2,1,0:T(8,128)(2,1)} %convert_element_type.101.refs_0_), custom_call_target="tpu_custom_call" | custom-call | tf_op jit(solution)/shard_map/pallas_call | solution.py:265
  75.8 5.4 %convolution_convert_fusion.1 = bf16[384,2048]{1,0:T(8,128)(2,1)} fusion(bf16[384,1024]{1,0:T(8,128)(2,1)} %bitcast.75, bf16[1024,2048]{1,0:T(8,128)(2,1)} %param.13), kind=kOutput, calls=%fused_computation.8 | convolution fusion | flops 1611399168 | bytes 6553600 | tf_op jit(solution)/shard_map/dot_general | solution.py:320
  81.2 0.0 copy-start.4
  81.2 22.9 %shard_map.95 = f32[1,48,2048]{2,1,0:T(8,128)} custom-call(bf16[8,48,2048]{2,1,0:T(8,128)(2,1)} %bitcast.72), custom_call_target="tpu_custom_call" | custom-call | tf_op jit(solution)/shard_map/pallas_call | solution.py:265
  104.2 0.0 copy-done.4
  104.2 1.7 fusion.31.refs_0_
  105.9 22.3 %shard_map.96 = bf16[8,48,2048]{2,1,0:T(8,128)(2,1)} custom-call(bf16[1,48,2048]{2,1,0:T(8,128)(2,1)} %fusion.31.refs_0_), custom_call_target="tpu_custom_call" | custom-call | tf_op jit(solution)/shard_map/pallas_call | solution.py:265
  128.2 0.0 copy-start
  128.2 1.9 multiply_reduce_fusion
  130.1 0.0 copy-done
  130.1 0.5 fusion.1.refs_2_
  130.6 0.0 copy-start.2
  130.6 0.1 broadcast_in_dim.33
  130.7 1.0 broadcast_in_dim.34.refs_1_
  131.7 10.9 %convolution_convert_fusion = bf16[384,3072]{1,0:T(8,128)(2,1)} fusion(bf16[384,2048]{1,0:T(8,128)(2,1)S(1)} %fusion.1.refs_2_, bf16[2048,3072]{1,0:T(8,128)(2,1)} %param.15), kind=kOutput, calls=%fused_computation.1 | convolution fusion | flops 4833017856 | bytes 16515072 | tf_op jit(solution)/shard_map/dot_general | solution.py:320
  142.5 0.0 copy-done.2
  142.5 37.8 %shard_map.97 = (f32[1,96,3072]{2,1,0:T(8,128)}, f32[1,96,128]{2,1,0:T(8,128)}, f32[1,96,3072]{2,1,0:T(8,128)}) custom-call(bf16[4,96,3072]{2,1,0:T(8,128)(2,1)} %bitcast.69, f32[4,96,128]{2,1,0:T(8,128)} %broadcast_in_dim.34.refs_1_, bf16[384,2048]{1,0:T(8,128)(2,1)} %copy-done.2, bf16[2048,3072]{1,0:T(8,128)(2,1)} %refs_3_.1), custom_call_target="tpu_custom_call" | custom-call | tf_op jit(solution)/shard_map/pallas_call | solution.py:265
  180.3 0.9 fusion.22
  181.3 2.9 %multiply_convert_fusion.refs_0_ = bf16[1,96,3072]{2,1,0:T(8,128)(2,1)} fusion(f32[1,96,3072]{2,1,0:T(8,128)} %get-tuple-element.20, f32[1,96,3072]{2,1,0:T(8,128)} %get-tuple-element.19, f32[96]{0:T(128)S(1)} %fusion.22), kind=kLoop, calls=%fused_computation.16 | loop fusion | flops 2359296 | bytes 2949504 | tf_op jit(solution)/shard_map/convert_element_type | solution.py:392
  184.1 19.8 %shard_map.98 = bf16[4,96,3072]{2,1,0:T(8,128)(2,1)} custom-call(bf16[1,96,3072]{2,1,0:T(8,128)(2,1)} %multiply_convert_fusion.refs_0_), custom_call_target="tpu_custom_call" | custom-call | tf_op jit(solution)/shard_map/pallas_call | solution.py:265
  203.9 9.7 %convolution_convert_fusion.2 = bf16[384,2048]{1,0:T(8,128)(2,1)} fusion(bf16[384,3072]{1,0:T(8,128)(2,1)} %bitcast.68, bf16[3072,2048]{1,0:T(8,128)(2,1)} %param.17), kind=kOutput, calls=%fused_computation.9 | convolution fusion | flops 4832624640 | bytes 16515072 | tf_op jit(solution)/shard_map/dot_general | solution.py:320
  213.6 0.0 copy-start.3
  213.6 22.5 %shard_map.99 = f32[1,48,2048]{2,1,0:T(8,128)} custom-call(bf16[8,48,2048]{2,1,0:T(8,128)(2,1)} %bitcast.73), custom_call_target="tpu_custom_call" | custom-call | tf_op jit(solution)/shard_map/pallas_call | solution.py:265
  236.1 0.0 copy-done.3
  236.1 1.7 fusion.12
  (3 shorter events, 0.0 us)
Async XLA Ops:
  26.2 1.9 copy-start.1
  60.2 1.5 copy-start.5
  61.7 1.6 copy-start.6
  81.2 22.9 %copy-start.4 = (bf16[48,2048]{1,0:T(8,128)(2,1)S(1)}, bf16[48,2048]{1,0:T(8,128)(2,1)}, u32[]{:S(2)}) copy-start(bf16[48,2048]{1,0:T(8,128)(2,1)} %param.9) | copy-start | bytes 589828
  128.2 1.9 copy-start
  130.6 11.9 %copy-start.2 = (bf16[384,2048]{1,0:T(8,128)(2,1)}, bf16[384,2048]{1,0:T(8,128)(2,1)S(1)}, u32[]{:S(2)}) copy-start(bf16[384,2048]{1,0:T(8,128)(2,1)S(1)} %fusion.1.refs_2_) | copy-start | bytes 4718596
  213.6 22.5 %copy-start.3 = (f32[1,48,2048]{2,1,0:T(8,128)S(1)}, f32[1,48,2048]{2,1,0:T(8,128)}, u32[]{:S(2)}) copy-start(f32[1,48,2048]{2,1,0:T(8,128)} %shard_map.95) | copy-start | bytes 1179652
